TPU v7x, 512 devices: a whole 4x4x16 slice. The times are simulated.
512 devices in a mesh: ctx: 32 (over z, x_lo), zero: 16 (over x_hi, y, core).
Axes of the slice: x: 4 (x_hi: 2, x_lo: 2; x = x_hi * 2 + x_lo), y: 4, z: 16, core: 2. Of those that a mesh axis runs over, the one named last changes fastest.
Arguments:
- activations: bfloat16 [16384, 4096], P('ctx', 'zero'), may hold values from -1200 to 1200
- norm_gain: bfloat16 [4096], replicated, may hold values from 0.099609375 to 1.8984375
- query_weight: bfloat16 [4096, 4096], P('ctx', 'zero'), may hold values from -24 to 24
- kv_weight: bfloat16 [4096, 16, 128], P('ctx', 'zero'), may hold values from -1 to 1
- out_weight: bfloat16 [4096, 4096], P('zero', 'ctx'), may hold values from -0.09375 to 0.09375
- tile_mask: int32 [32, 4, 4], P('ctx'), may hold values from 0 to 1, as said below
- anchor_mask: int32 [32, 4, 4], P('ctx'), may hold values 0 or 1
- anchor_index: int32 [1], replicated, may hold values from 0 to 31
Outputs:
- mixed: bfloat16 [16384, 4096], P(('ctx', 'zero'))
Inputs may be any that keep to these rules, and one draw needn't show every extreme that they name: `tile_mask`: entries of every block's table above the diagonal are 0 and diagonal entries are 1.
All inputs are finite; a program needn't handle non-finite values. No bound on the sum of `anchor_mask` on one device may be relied on, other than what follows from the above.
Results may differ from a plain program's by a relative error of at most 0.02.
Values may be sent and summed in bfloat16 or wider, within the bound.
A program may use at most 64 MiB of HBM per device.

v0:
```python
import jax
import jax.numpy as jnp
from jax import lax
from jax.sharding import PartitionSpec as P


def from_partner(value, axis, stride):
    mask = 2**stride
    pairs = [(source, source ^ mask) for source in range(lax.axis_size(axis))]
    return lax.ppermute(value, axis, pairs)


def from_root(block, axis, holder):
    block = jnp.where(lax.axis_index(axis) == holder, block, jnp.zeros_like(block))
    return lax.psum(block, axis)


def rotate(vectors, positions):
    half_size = vectors.shape[-1] // 2
    frequency = jnp.power(
        jnp.float32(500000.0), -(jnp.arange(half_size, dtype=jnp.float32) * 2.0 / vectors.shape[-1])
    )
    angles = positions.astype(jnp.float32)[:, None] * frequency[None, :]
    cosine_table = jnp.cos(angles)[:, None, :]
    sine_table = jnp.sin(angles)[:, None, :]
    first = vectors[..., :half_size]
    second = vectors[..., half_size:]
    return jnp.concatenate(
        [first * cosine_table - second * sine_table, second * cosine_table + first * sine_table], -1
    )


def expand_tiles(table, tile_size):
    tiles = table.shape[0]
    return jnp.broadcast_to(table[:, None, :, None], (tiles, tile_size, tiles, tile_size)).reshape(
        tiles * tile_size, tiles * tile_size
    )


def local(
    activations,
    norm_gain,
    query_weight,
    kv_weight,
    out_weight,
    tile_mask,
    anchor_mask,
    anchor_index,
):
    block_rows = activations.shape[0]
    head_size = kv_weight.shape[2]
    zero_rank = lax.axis_index("zero")
    ctx_rank = lax.axis_index("ctx")
    gain_float = norm_gain.astype(jnp.float32)
    gathered = lax.all_gather(activations, "zero", axis=1, tiled=True)
    x_float = gathered.astype(jnp.float32)
    mean_square = jnp.mean(x_float * x_float, -1, keepdims=True)
    normed = (x_float * lax.rsqrt(mean_square + 1e-05) * gain_float).astype(jnp.bfloat16)
    kv_rows_local = kv_weight[:, 0, :]

    def add_one(piece_rows):
        return jnp.dot(normed, piece_rows, preferred_element_type=jnp.float32)

    query_linear = add_one(lax.all_gather(query_weight, "ctx", axis=0, tiled=True))
    kv_linear = add_one(lax.all_gather(kv_rows_local, "ctx", axis=0, tiled=True))
    positions = ctx_rank * block_rows + jnp.arange(block_rows, dtype=jnp.int32)
    queries = (
        rotate(query_linear.reshape(block_rows, -1, head_size), positions) * head_size ** (-0.5)
    ).astype(jnp.bfloat16)
    is_key = zero_rank % 2 == 0
    own_half = jnp.where(
        is_key, rotate(kv_linear[:, None, :], positions)[:, 0, :], kv_linear
    ).astype(jnp.bfloat16)
    partner = from_partner(own_half, "zero", 0)
    own_keys = jnp.where(is_key, own_half, partner)
    own_values = jnp.where(is_key, partner, own_half)
    anchor_block = anchor_index[0]
    anchor_pair = from_root(jnp.stack([own_keys, own_values]), "ctx", anchor_block)
    all_keys = jnp.concatenate([anchor_pair[0], own_keys], 0)
    all_values = jnp.concatenate([anchor_pair[1], own_values], 0)
    scores = jnp.einsum("thd,kd->htk", queries, all_keys, preferred_element_type=jnp.float32)
    tile_size = block_rows // tile_mask.shape[1]
    row_offsets = jnp.arange(block_rows, dtype=jnp.int32)
    far_visible = (expand_tiles(anchor_mask[0], tile_size) == 1) & (ctx_rank != anchor_block)
    near_visible = (expand_tiles(tile_mask[0], tile_size) == 1) & (
        row_offsets[None, :] <= row_offsets[:, None]
    )
    visible = jnp.concatenate([far_visible, near_visible], 1)[None]
    scores = jnp.where(visible, scores, jnp.float32(-1e30))
    largest = jnp.max(scores, -1, keepdims=True)
    weights = jnp.where(visible, jnp.exp(scores - largest), jnp.float32(0.0))
    row_total = jnp.sum(weights, -1)
    rounded = weights.astype(jnp.bfloat16)
    attended = (
        jnp.einsum("htk,kd->thd", rounded, all_values, preferred_element_type=jnp.float32)
        / jnp.transpose(row_total)[:, :, None]
    )
    attended = attended.astype(jnp.bfloat16).reshape(block_rows, -1)
    out_rows = lax.all_gather(out_weight, "ctx", axis=1, tiled=True)
    return lax.psum_scatter(
        jnp.dot(attended, out_rows, preferred_element_type=jnp.float32).astype(jnp.bfloat16),
        "zero",
        scatter_dimension=0,
        tiled=True,
    )


def solution(mesh):
    placed = (
        P("ctx", "zero"),
        P(),
        P("ctx", "zero"),
        P("ctx", "zero", None),
        P("zero", "ctx"),
        P("ctx", None, None),
        P("ctx", None, None),
        P(),
    )
    return jax.shard_map(
        local, mesh=mesh, in_specs=placed, out_specs=P(("ctx", "zero"), None), check_vma=False
    )
```

profile of v0, /device:TPU:32, one launch (start us, length us, event | category | flops | bytes accessed | tf_op | source)
XLA Modules:
  0.0 865.7 jit_solution(16125754676907653811)
XLA Ops:
  6.5 0.7 all-gather.6.cloned.1.call-update
  7.3 0.7 all-gather.12.cloned.1.call-update
  8.1 0.7 all-gather.8.cloned.1.call-update
  8.8 0.7 convert_element_type.33
  9.5 76.8 %all-gather.6.cloned.1.call-done = bf16[512,4096]{1,0:T(8,128)(2,1)} async-done(((bf16[512,256]{1,0:T(8,128)(2,1)}), bf16[512,4096]{1,0:T(8,128)(2,1)}) %all-gather.6.cloned.1.call-update) | async-done | bytes 4194320 | tf_op jit(solution)/shard_map/all_gather | solution.py:55
  86.3 3.1 fusion.1
  89.4 127.2 %all-gather.12.cloned.1.call-done = bf16[4096,1,128]{2,0,1:T(8,128)(2,1)} async-done(((bf16[128,1,128]{2,0,1:T(8,128)(2,1)}), bf16[4096,1,128]{2,0,1:T(8,128)(2,1)}) %all-gather.12.cloned.1.call-update) | async-done | bytes 1048592 | tf_op jit(solution)/shard_map/all_gather | solution.py:65
  216.6 4.1 fusion.17
  220.7 0.6 fusion.36
  221.3 1.9 collective-permute-start
  223.9 0.7 collective-permute-done
  224.6 0.7 maximum_select_fusion
  225.4 0.5 all-gather.10.cloned.1.call-update
  226.1 0.2 broadcast_in_dim.24
  227.0 1.0 multiply_cosine_fusion
  228.0 122.4 %all-gather.8.cloned.1.call-done = bf16[4096,256]{1,0:T(8,128)(2,1)} async-done(((bf16[128,256]{1,0:T(8,128)(2,1)}), bf16[4096,256]{1,0:T(8,128)(2,1)}) %all-gather.8.cloned.1.call-update) | async-done | bytes 2097168 | tf_op jit(solution)/shard_map/all_gather | solution.py:64
  350.4 4.4 fusion.15
  355.4 260.9 %all-reduce.2.cloned.1.call-done = bf16[2,512,128]{1,2,0:T(8,128)(2,1)} async-done(((bf16[2,512,128]{1,2,0:T(8,128)(2,1)}), bf16[2,512,128]{1,2,0:T(8,128)(2,1)}) %all-reduce.2.cloned.1.call-update) | async-done | bytes 262160 | tf_op jit(solution)/shard_map/psum | solution.py:15
  616.3 1.0 slice_bitcast_fusion.1
  617.2 3.5 fusion.45
  620.7 2.0 fusion.19
  622.8 129.2 %all-gather.10.cloned.1.call-done = bf16[256,4096]{1,0:T(8,128)(2,1)} async-done(((bf16[256,128]{1,0:T(8,128)(2,1)}), bf16[256,4096]{1,0:T(8,128)(2,1)}) %all-gather.10.cloned.1.call-update) | async-done | bytes 2097168 | tf_op jit(solution)/shard_map/all_gather | solution.py:99
  752.0 4.8 convolution_convert_fusion
  756.9 102.0 %reduce-scatter.2.cloned.1.call-done = bf16[32,4096]{1,0:T(8,128)(2,1)} async-done(((bf16[512,4096]{1,0:T(8,128)(2,1)}), bf16[32,4096]{1,0:T(8,128)(2,1)}) %reduce-scatter.2.cloned.1.call-update) | async-done | bytes 262160 | tf_op jit(solution)/shard_map/reduce_scatter | solution.py:100
  (29 shorter events, 1.6 us)
Async XLA Ops:
  6.5 79.8 %all-gather.6.cloned.1.call-start = ((), (), s32[]{:S(2)}) async-start(), calls=%async_computation.1 | async-start | bytes 4456448 | tf_op jit(solution)/shard_map/all_gather | solution.py:55
  7.3 209.4 %all-gather.12.cloned.1.call-start = ((), (), s32[]{:S(2)}) async-start(), calls=%async_computation.6 | async-start | bytes 1081344 | tf_op jit(solution)/shard_map/all_gather | solution.py:65
  8.0 342.4 %all-gather.8.cloned.1.call-start = ((), (), s32[]{:S(2)}) async-start(), calls=%async_computation.3 | async-start | bytes 2162688 | tf_op jit(solution)/shard_map/all_gather | solution.py:64
  8.7 607.5 %all-reduce.2.cloned.1.call-start = ((), (), s32[]{:S(2)}) async-start(), calls=%async_computation.2 | async-start | bytes 524288 | tf_op jit(solution)/shard_map/psum | solution.py:15
  89.4 136.6 %copy-start.1 = (s32[1,4,4]{2,1,0:T(4,128)S(1)}, s32[1,4,4]{2,1,0:T(4,128)}, u32[]{:S(2)}) copy-start(s32[1,4,4]{2,1,0:T(4,128)} %param.14) | copy-start | bytes 196
  89.4 137.0 %copy-start = (s32[1,4,4]{2,1,0:T(4,128)S(1)}, s32[1,4,4]{2,1,0:T(4,128)}, u32[]{:S(2)}) copy-start(s32[1,4,4]{2,1,0:T(4,128)} %param.13) | copy-start | bytes 196
  221.3 3.2 collective-permute-start
  225.3 526.7 %all-gather.10.cloned.1.call-start = ((), (), s32[]{:S(2)}) async-start(), calls=%async_computation.4 | async-start | bytes 2162688 | tf_op jit(solution)/shard_map/all_gather | solution.py:99
  225.9 632.9 %reduce-scatter.2.cloned.1.call-start = ((), (), s32[]{:S(2)}) async-start(), calls=%async_computation.5 | async-start | bytes 4456448 | tf_op jit(solution)/shard_map/reduce_scatter | solution.py:100
Sparse Core Ops, SparseCore 0:
  10.5 75.8 all-gather.5
  88.4 128.1 all-gather.11
  218.7 131.6 all-gather.7
  353.1 263.0 all-reduce.1
  618.1 133.8 all-gather.9
  757.0 101.8 reduce-scatter.1
where the time goes:
time: 866 us
  waiting for transfers between devices  822 us (95%)
  matrix products  18.9 us (2%)
  between operations  14.3 us (2%)
    psum x1, waiting for transfers between devices, from_root(): return lax.psum(block, axis)  261 us
    all_gather x1, waiting for transfers between devices, local(): out_rows = lax.all_gather(out_weight, 'ctx', axis=1, tiled=True)  129 us
    all_gather x1, waiting for transfers between devices, local(): lax.all_gather(kv_rows_local, 'ctx', axis=0, tiled=True)  127 us
    all_gather x1, waiting for transfers between devices, local(): lax.all_gather(query_weight, 'ctx', axis=0, tiled=True)  122 us
    reduce_scatter x1, waiting for transfers between devices, local(): lax.psum_scatter(jnp.dot(attended, out_rows, preferred_element_type=jnp.f...  102 us
    all_gather x1, waiting for transfers between devices, local(): gathered = lax.all_gather(activations, 'zero', axis=1, tiled=True)  76.8 us
  transfers between devices with their start and end apart: 7, of which 7 were waited for; matrix products, arithmetic and copies ran while one was open for 3% of the time, Pallas kernels for 0%

commit v1 on v0

--- a/solution.py
+++ b/solution.py
@@ -62,7 +62,11 @@
         return jnp.dot(normed, piece_rows, preferred_element_type=jnp.float32)
 
     query_linear = add_one(lax.all_gather(query_weight, "ctx", axis=0, tiled=True))
-    kv_linear = add_one(lax.all_gather(kv_rows_local, "ctx", axis=0, tiled=True))
+    kv_linear = add_one(
+        jnp.concatenate(
+            lax.all_to_all(jnp.stack([kv_rows_local] * lax.axis_size("ctx")), "ctx", 0, 0), axis=0
+        )
+    )
     positions = ctx_rank * block_rows + jnp.arange(block_rows, dtype=jnp.int32)
     queries = (
         rotate(query_linear.reshape(block_rows, -1, head_size), positions) * head_size ** (-0.5)

time: 866 us -> 736 us (0.85)
  waiting for transfers between devices: 822 us -> 674 us
  starting transfers between devices: 2.12 us -> 18.6 us
    all_gather x1 -> x0, waiting for transfers between devices: 127 us -> none  [local(): lax.all_gather(kv_rows_local, 'ctx', axis=0, tiled=True)]
    all_to_all x0 -> x1, starting transfers between devices: none -> 16.3 us  [local(): lax.all_to_all(jnp.stack([kv_rows_local] * lax.axis_size('ctx')), 'ctx',...]
    all_gather x1, waiting for transfers between devices: 76.8 us -> 61.6 us  [local(): gathered = lax.all_gather(activations, 'zero', axis=1, tiled=True)]
  transfers between devices with their start and end apart: 7 -> 7, of which waited for: 7 -> 6; matrix products, arithmetic and copies ran while one was open for 3% -> 3% of each run, Pallas kernels for 0% -> 0%
where the time goes in v1:
time: 736 us
  waiting for transfers between devices  674 us (92%)
  starting transfers between devices  18.6 us (3%)
  matrix products  18.6 us (3%)
  between operations  14 us (2%)
    psum x1, waiting for transfers between devices, from_root(): return lax.psum(block, axis)  261 us
    all_gather x1, waiting for transfers between devices, local(): out_rows = lax.all_gather(out_weight, 'ctx', axis=1, tiled=True)  129 us
    all_gather x1, waiting for transfers between devices, local(): lax.all_gather(query_weight, 'ctx', axis=0, tiled=True)  118 us
    reduce_scatter x1, waiting for transfers between devices, local(): lax.psum_scatter(jnp.dot(attended, out_rows, preferred_element_type=jnp.f...  102 us
    all_gather x1, waiting for transfers between devices, local(): gathered = lax.all_gather(activations, 'zero', axis=1, tiled=True)  61.6 us
    all_to_all x1, starting transfers between devices, local(): lax.all_to_all(jnp.stack([kv_rows_local] * lax.axis_size('ctx')), 'ctx',...  16.3 us
  transfers between devices with their start and end apart: 7, of which 6 were waited for; matrix products, arithmetic and copies ran while one was open for 3% of the time, Pallas kernels for 0%

profile of v1, /device:TPU:32, one launch (start us, length us, event | category | flops | bytes accessed | tf_op | source)
XLA Modules:
  0.0 735.9 jit_solution(4992441169461607743)
XLA Ops:
  6.5 0.7 all-gather.4.cloned.1.call-update
  7.3 2.0 stack.12
  9.2 16.3 %all-to-all-start = ((bf16[32,128,128]{2,1,0:T(8,128)(2,1)}), bf16[32,128,128]{2,1,0:T(8,128)(2,1)S(1)}, u32[]{:S(2)}, u32[]{:S(2)}) async-start(bf16[32,128,128]{2,1,0:T(8,128)(2,1)} %stack.12), calls=%async_computation | async-start | bytes 2097152 | tf_op jit(solution)/shard_map/all_to_all | solution.py:67
  25.6 0.7 all-gather.6.cloned.1.call-update
  26.3 0.7 convert_element_type.33
  27.0 61.6 %all-gather.4.cloned.1.call-done = bf16[512,4096]{1,0:T(8,128)(2,1)} async-done(((bf16[512,256]{1,0:T(8,128)(2,1)}), bf16[512,4096]{1,0:T(8,128)(2,1)}) %all-gather.4.cloned.1.call-update) | async-done | bytes 4194320 | tf_op jit(solution)/shard_map/all_gather | solution.py:55
  88.6 3.1 fusion.1
  91.8 3.8 fusion.17
  95.6 0.6 fusion.35
  96.2 2.2 collective-permute-start
  99.0 0.4 collective-permute-done
  99.4 0.7 maximum_select_fusion
  100.2 0.5 all-gather.8.cloned.1.call-update
  101.0 0.2 broadcast_in_dim.24
  101.8 1.0 multiply_cosine_fusion
  102.8 117.8 %all-gather.6.cloned.1.call-done = bf16[4096,256]{1,0:T(8,128)(2,1)} async-done(((bf16[128,256]{1,0:T(8,128)(2,1)}), bf16[4096,256]{1,0:T(8,128)(2,1)}) %all-gather.6.cloned.1.call-update) | async-done | bytes 2097168 | tf_op jit(solution)/shard_map/all_gather | solution.py:64
  220.7 4.4 fusion.15
  225.7 261.0 %all-reduce.2.cloned.1.call-done = bf16[2,512,128]{1,2,0:T(8,128)(2,1)} async-done(((bf16[2,512,128]{1,2,0:T(8,128)(2,1)}), bf16[2,512,128]{1,2,0:T(8,128)(2,1)}) %all-reduce.2.cloned.1.call-update) | async-done | bytes 262160 | tf_op jit(solution)/shard_map/psum | solution.py:15
  486.7 1.0 slice_bitcast_fusion.1
  487.7 3.5 fusion.44
  491.2 2.0 fusion.19
  493.2 129.2 %all-gather.8.cloned.1.call-done = bf16[256,4096]{1,0:T(8,128)(2,1)} async-done(((bf16[256,128]{1,0:T(8,128)(2,1)}), bf16[256,4096]{1,0:T(8,128)(2,1)}) %all-gather.8.cloned.1.call-update) | async-done | bytes 2097168 | tf_op jit(solution)/shard_map/all_gather | solution.py:103
  622.5 4.8 convolution_convert_fusion
  627.3 102.0 %reduce-scatter.2.cloned.1.call-done = bf16[32,4096]{1,0:T(8,128)(2,1)} async-done(((bf16[512,4096]{1,0:T(8,128)(2,1)}), bf16[32,4096]{1,0:T(8,128)(2,1)}) %reduce-scatter.2.cloned.1.call-update) | async-done | bytes 262160 | tf_op jit(solution)/shard_map/reduce_scatter | solution.py:104
  (29 shorter events, 1.6 us)
Async XLA Ops:
  6.5 82.1 %all-gather.4.cloned.1.call-start = ((), (), s32[]{:S(2)}) async-start(), calls=%async_computation.2 | async-start | bytes 4456448 | tf_op jit(solution)/shard_map/all_gather | solution.py:55
  9.2 82.5 %all-to-all-start = ((bf16[32,128,128]{2,1,0:T(8,128)(2,1)}), bf16[32,128,128]{2,1,0:T(8,128)(2,1)S(1)}, u32[]{:S(2)}, u32[]{:S(2)}) async-start(bf16[32,128,128]{2,1,0:T(8,128)(2,1)} %stack.12), calls=%async_computation | async-start | bytes 2097152 | tf_op jit(solution)/shard_map/all_to_all | solution.py:67
  25.5 195.1 %all-gather.6.cloned.1.call-start = ((), (), s32[]{:S(2)}) async-start(), calls=%async_computation.4 | async-start | bytes 2162688 | tf_op jit(solution)/shard_map/all_gather | solution.py:64
  26.3 460.4 %all-reduce.2.cloned.1.call-start = ((), (), s32[]{:S(2)}) async-start(), calls=%async_computation.3 | async-start | bytes 524288 | tf_op jit(solution)/shard_map/psum | solution.py:15
  91.7 9.1 %copy-start.1 = (s32[1,4,4]{2,1,0:T(4,128)S(1)}, s32[1,4,4]{2,1,0:T(4,128)}, u32[]{:S(2)}) copy-start(s32[1,4,4]{2,1,0:T(4,128)} %param.14) | copy-start | bytes 196
  91.7 9.6 %copy-start = (s32[1,4,4]{2,1,0:T(4,128)S(1)}, s32[1,4,4]{2,1,0:T(4,128)}, u32[]{:S(2)}) copy-start(s32[1,4,4]{2,1,0:T(4,128)} %param.13) | copy-start | bytes 196
  96.2 3.2 collective-permute-start
  100.2 522.3 %all-gather.8.cloned.1.call-start = ((), (), s32[]{:S(2)}) async-start(), calls=%async_computation.5 | async-start | bytes 2162688 | tf_op jit(solution)/shard_map/all_gather | solution.py:103
  100.8 628.6 %reduce-scatter.2.cloned.1.call-start = ((), (), s32[]{:S(2)}) async-start(), calls=%async_computation.6 | async-start | bytes 4456448 | tf_op jit(solution)/shard_map/reduce_scatter | solution.py:104
Sparse Core Ops, SparseCore 0:
  10.5 78.1 all-gather.3
  90.7 129.8 all-gather.5
  223.6 263.0 all-reduce.1
  488.6 133.8 all-gather.7
  627.5 101.8 reduce-scatter.1
